TPU v7x, 32 devices: a whole 2x2x4 slice. The times are simulated.
32 devices in a mesh: ma: 8 (over z, y), freq: 4 (over x, core).
Axes of the slice: x: 2, y: 2, z: 4, core: 2. Of those that a mesh axis runs over, the one named last changes fastest.
Arguments:
- visibility: float32 [2, 128, 16, 12288], P(None, None, 'ma', 'freq'), may hold values from -6 to 6
- svd_ranks: int32 [64], P('freq'), may hold values from 96 to 192, as said below
- kl_basis: bfloat16 [2, 12288, 1024], P(None, 'freq'), may hold values from -0.0390625 to 0.0390625
- weight_table: float32 [8, 1024], replicated, may hold values from 0.5 to 5
- seed_labels: int32 [128], replicated, may hold values from 0 to 7
Outputs:
- time_series: float32 [2, 128, 16, 12288], P(None, 'ma', None, 'freq')
Inputs may be any that keep to these rules, and one draw needn't show every extreme that they name: `svd_ranks`: some frequency has all 192 components.
All inputs are finite; a program needn't handle non-finite values.
Results may differ from a plain program's by a relative error of at most 0.004.
Values may be sent and summed in bfloat16 or wider, within the bound.
No kernel may reach another device: no remote copies, remote signals or barrier semaphores. Data moves between devices by JAX's collectives and lax.ppermute only.
A program may use at most 64 MiB of HBM per device.

v0:
```python
import math
import jax
import jax.numpy as jnp
from jax import lax
from jax.sharding import PartitionSpec as P

S = 192
contract_first = (((0,), (1,)), ((), ()))


def product(matrix, signal):
    return lax.dot_general(matrix, signal, contract_first, preferred_element_type=jnp.float32)


def mode_terms(masked_re, masked_im, kl_basis):
    modes_re = product(kl_basis[0], masked_re) + product(kl_basis[1], masked_im)
    modes_im = product(kl_basis[0], masked_im) - product(kl_basis[1], masked_re)
    return jnp.stack([modes_re, modes_im], axis=1)


def add_modes(pieces, kl_basis):
    new_re = product(pieces[:, 0], kl_basis[0]) - product(pieces[:, 1], kl_basis[1])
    new_im = product(pieces[:, 0], kl_basis[1]) + product(pieces[:, 1], kl_basis[0])
    return (new_re, new_im)


def to_times(fields):
    mode_length = fields.shape[2]
    mode_index = jnp.arange(mode_length, dtype=jnp.int32)
    phase_steps = mode_index[:, None] * mode_index[None, :] % mode_length
    angles = phase_steps.astype(jnp.float32) * (2.0 * math.pi / mode_length)
    cosine_table = jnp.cos(angles) / math.sqrt(mode_length)
    sine_table = jnp.sin(angles) / math.sqrt(mode_length)

    def apply_table(matrix, signal):
        return jnp.einsum("tm,rmc->rtc", matrix, signal, precision=lax.Precision.HIGHEST)

    series_re = apply_table(cosine_table, fields[0]) - apply_table(sine_table, fields[1])
    series_im = apply_table(sine_table, fields[0]) + apply_table(cosine_table, fields[1])
    return jnp.stack([series_re, series_im])


def shards(visibility, svd_ranks, kl_basis, weight_table, seed_labels):
    real_count = visibility.shape[1]
    local_m = visibility.shape[2]
    columns_dev = visibility.shape[3]
    row_total = real_count * local_m
    freq_dev = svd_ranks.shape[0]
    column_mask = (jnp.arange(S, dtype=jnp.int32)[None, :] < svd_ranks[:, None]).astype(jnp.float32)
    column_mask = column_mask.reshape(1, 1, 1, freq_dev * S)
    masked = (visibility * column_mask).astype(jnp.bfloat16).reshape(2, row_total, columns_dev)
    masked_re = masked[0]
    masked_im = masked[1]
    mode_total = kl_basis.shape[2]
    share_modes = mode_total // lax.axis_size("freq")
    summed = lax.psum_scatter(
        mode_terms(masked_re, masked_im, kl_basis), "freq", scatter_dimension=0, tiled=True
    )
    first_mode = lax.axis_index("freq") * share_modes
    held_modes = summed.shape[0]
    set_count = weight_table.shape[0]
    seed_rows = jnp.repeat(seed_labels, local_m)
    one_hot = (jnp.arange(set_count, dtype=jnp.int32)[:, None] == seed_rows[None, :]).astype(
        jnp.float32
    )
    table_part = lax.dynamic_slice_in_dim(weight_table, first_mode, held_modes, 1)
    row_weights = lax.dot_general(
        table_part, one_hot, (((0,), (0,)), ((), ())), precision=lax.Precision.HIGHEST
    )
    coeffs = (summed * row_weights[:, None, :]).astype(jnp.bfloat16)
    coeffs = lax.all_to_all(
        coeffs.reshape(held_modes, 2, real_count, local_m),
        "ma",
        split_axis=2,
        concat_axis=3,
        tiled=True,
    )
    coeffs = coeffs.reshape(held_modes, 2, -1)
    fields_re, fields_im = add_modes(lax.all_gather(coeffs, "freq", axis=0, tiled=True), kl_basis)
    fields = jnp.stack([fields_re, fields_im])
    return to_times(fields.reshape(2, real_count // lax.axis_size("ma"), -1, columns_dev))


def solution(mesh):
    in_specs = (P(None, None, "ma", "freq"), P("freq"), P(None, "freq", None), P(), P())
    out_specs = P(None, "ma", None, "freq")
    return jax.shard_map(shards, mesh=mesh, in_specs=in_specs, out_specs=out_specs, check_vma=False)
```

profile of v0, /device:TPU:0, one launch (start us, length us, event | category | flops | bytes accessed | tf_op | source)
XLA Modules:
  0.0 141.5 jit_solution(1786989514832228555)
XLA Ops:
  6.5 0.0 reduce-scatter.2.cloned.1.call-start
  6.5 0.7 fusion.48
  7.3 0.1 reshape.42
  7.4 5.0 %multiply_convert_fusion = bf16[2,128,2,3072]{3,2,1,0:T(2,128)(2,1)S(1)} fusion(f32[2,128,2,3072]{3,2,1,0:T(2,128)} %param.5, f32[3072]{0:T(1024)S(1)} %reshape.42), kind=kLoop, calls=%fused_computation.17 | loop fusion | flops 3145728 | bytes 9449472 | tf_op jit(solution)/shard_map/convert_element_type | solution.py:51
  12.3 2.2 %fusion.93 = (bf16[1,128,2,3072]{3,2,1,0:T(2,128)(2,1)S(1)}, bf16[1,128,2,3072]{3,2,1,0:T(2,128)(2,1)S(1)}) fusion(bf16[2,128,2,3072]{3,2,1,0:T(2,128)(2,1)S(1)} %multiply_convert_fusion), kind=kLoop, calls=%fused_computation.90 | loop fusion | bytes 6291456 | tf_op jit(solution)/shard_map/slice | solution.py:53
  14.5 1.5 %squeeze.36 = bf16[256,3072]{1,0:T(8,128)(2,1)} reshape(bf16[1,128,2,3072]{3,2,1,0:T(2,128)(2,1)S(1)} %get-tuple-element.5) | data formatting | bytes 3145728 | tf_op jit(solution)/shard_map/squeeze | solution.py:53
  16.1 1.5 %squeeze.16 = bf16[256,3072]{1,0:T(8,128)(2,1)} reshape(bf16[1,128,2,3072]{3,2,1,0:T(2,128)(2,1)S(1)} %get-tuple-element.6) | data formatting | bytes 3145728 | tf_op jit(solution)/shard_map/squeeze | solution.py:52
  17.6 0.3 copy-done.2
  17.9 4.7 %fusion.6 = f32[256,1024]{1,0:T(8,128)S(1)} fusion(bf16[256,3072]{1,0:T(8,128)(2,1)S(1)} %copy-done.2, bf16[2,3072,1024]{2,1,0:T(8,128)(2,1)} %param.7), kind=kOutput, calls=%fused_computation.7 | convolution fusion | flops 1610612736 | bytes 8912896 | tf_op jit(solution)/shard_map/dot_general | solution.py:12
  22.6 0.0 slice-start.2
  22.6 4.7 %fusion.4 = f32[256,1024]{1,0:T(8,128)S(1)} fusion(bf16[256,3072]{1,0:T(8,128)(2,1)S(1)} %copy-done.3, bf16[2,3072,1024]{2,1,0:T(8,128)(2,1)} %param.7), kind=kOutput, calls=%fused_computation.5 | convolution fusion | flops 1610612736 | bytes 8912896 | tf_op jit(solution)/shard_map/dot_general | solution.py:12
  27.4 1.8 %fusion.35 = f32[1024,1,256]{0,2,1:T(8,128)S(1)} fusion(f32[256,1024]{1,0:T(8,128)S(1)} %fusion.6, bf16[256,3072]{1,0:T(8,128)(2,1)S(1)} %copy-done.3, bf16[2,3072,1024]{2,1,0:T(8,128)(2,1)S(1)} %bitcast.87), kind=kOutput, calls=%fused_computation.34 | convolution fusion | flops 1610874880 | bytes 9961472 | tf_op jit(solution)/shard_map/dot_general | solution.py:12
  29.2 1.8 %fusion.41 = f32[1024,1,256]{0,2,1:T(8,128)S(1)} fusion(f32[256,1024]{1,0:T(8,128)S(1)} %fusion.4, bf16[256,3072]{1,0:T(8,128)(2,1)S(1)} %copy-done.2, bf16[2,3072,1024]{2,1,0:T(8,128)(2,1)S(1)} %bitcast.87), kind=kOutput, calls=%fused_computation.36 | convolution fusion | flops 1610874880 | bytes 9961472 | tf_op jit(solution)/shard_map/dot_general | solution.py:12
  31.0 0.0 copy-start.4
  31.0 1.5 %pad_maximum_fusion.1 = f32[1024,2,256]{0,2,1:T(8,128)} fusion(f32[1024,1,256]{0,2,1:T(8,128)S(1)} %fusion.41, f32[1024,1,256]{0,2,1:T(8,128)S(1)} %fusion.35), kind=kLoop, calls=%fused_computation.32 | loop fusion | flops 524288 | bytes 4194304 | tf_op jit(solution)/shard_map/stack | solution.py:18
  32.5 0.0 reduce-scatter.2.cloned.1.call-update
  32.5 0.0 all-gather.2.cloned.1.call-start
  32.5 0.1 broadcast_in_dim.2
  32.6 0.1 eq.18
  32.8 0.0 copy-done
  32.8 0.3 fusion.60
  33.1 33.4 %reduce-scatter.2.cloned.1.call-done = f32[256,2,256]{0,2,1:T(8,128)} async-done(((f32[1024,2,256]{0,2,1:T(8,128)}), f32[256,2,256]{0,2,1:T(8,128)}) %reduce-scatter.2.cloned.1.call-update) | async-done | bytes 524304 | tf_op jit(solution)/shard_map/reduce_scatter | solution.py:56
  66.5 1.1 multiply_convert_fusion.1
  67.6 0.1 reshape.40
  67.7 0.2 copy.16
  67.9 14.1 %all_to_all.15 = bf16[256,2,128,2]{0,3,1,2:T(2,128)(2,1)S(1)} all-to-all(bf16[256,2,128,2]{0,3,1,2:T(2,128)(2,1)S(1)} %copy.16), channel_id=1, replica_groups=mesh['ma'=8,'freq'=4] {'ma'}, dimensions={2} | all-to-all | bytes 524288 | tf_op jit(solution)/shard_map/all_to_all | solution.py:71
  82.0 1.0 copy.18
  83.0 0.0 all-gather.2.cloned.1.call-update
  83.0 15.0 %all-gather.2.cloned.1.call-done = bf16[1024,2,256]{0,1,2:T(2,128)(2,1)} async-done(((bf16[256,2,256]{0,1,2:T(2,128)(2,1)}), bf16[1024,2,256]{0,1,2:T(2,128)(2,1)}) %all-gather.2.cloned.1.call-update) | async-done | bytes 1048592 | tf_op jit(solution)/shard_map/all_gather | solution.py:79
  98.1 3.4 %fusion.94 = (bf16[1024,1,256]{0,1,2:T(2,128)(2,1)S(1)}, bf16[1024,1,256]{0,1,2:T(2,128)(2,1)S(1)}) fusion(bf16[1024,2,256]{0,1,2:T(2,128)(2,1)} %all-gather.2.cloned.1.call-done), kind=kLoop, calls=%fused_computation.91 | loop fusion | bytes 2097152 | tf_op jit(solution)/shard_map/slice | solution.py:22
  101.5 0.9 copy.19
  102.4 1.1 copy.20
  103.5 0.0 slice-start.3
  103.5 0.0 slice-start.4
  103.6 4.8 %fusion.2 = f32[256,3072]{1,0:T(8,128)S(1)} fusion(bf16[2,3072,1024]{2,1,0:T(8,128)(2,1)} %param.7, bf16[1024,1,256]{2,0,1:T(8,128)(2,1)S(1)} %copy.20), kind=kOutput, calls=%fused_computation.3 | convolution fusion | flops 1610612736 | bytes 9961472 | tf_op jit(solution)/shard_map/dot_general | solution.py:12
  108.3 0.0 slice-start.5
  108.4 4.8 %fusion = f32[256,3072]{1,0:T(8,128)S(1)} fusion(bf16[2,3072,1024]{2,1,0:T(8,128)(2,1)} %param.7, bf16[1024,1,256]{2,0,1:T(8,128)(2,1)S(1)} %copy.19), kind=kOutput, calls=%fused_computation.1 | convolution fusion | flops 1610612736 | bytes 9961472 | tf_op jit(solution)/shard_map/dot_general | solution.py:12
  113.1 0.0 slice-done.3
  113.1 0.0 slice-done.4
  113.2 0.0 slice-done.5
  113.2 1.9 %fusion.26 = f32[256,3072]{1,0:T(8,128)S(1)} fusion(f32[256,3072]{1,0:T(8,128)S(1)} %fusion.2, bf16[2,3072,1024]{2,1,0:T(8,128)(2,1)S(1)} %bitcast.89, bf16[1024,1,256]{2,0,1:T(8,128)(2,1)S(1)} %copy.19), kind=kOutput, calls=%fused_computation.30 | convolution fusion | flops 1611399168 | bytes 13107200 | tf_op jit(solution)/shard_map/dot_general | solution.py:12
  115.1 3.4 %fusion.52 = f32[16,3072,16]{1,2,0:T(8,128)S(1)} fusion(f32[16,16,3072]{2,1,0:T(8,128)S(1)} %bitcast.82), kind=kOutput, calls=%fused_computation.50 | convolution fusion | flops 150998784 | bytes 6291456 | tf_op jit(solution)/shard_map/tm,rmc->rtc/dot_general | solution.py:36
  118.5 3.4 %fusion.56 = f32[16,3072,16]{1,2,0:T(8,128)S(1)} fusion(f32[16,16,3072]{2,1,0:T(8,128)S(1)} %bitcast.83), kind=kOutput, calls=%fused_computation.54 | convolution fusion | flops 150998784 | bytes 6291456 | tf_op jit(solution)/shard_map/tm,rmc->rtc/dot_general | solution.py:36
  121.9 2.2 %fusion.29 = f32[256,3072]{1,0:T(8,128)S(1)} fusion(f32[256,3072]{1,0:T(8,128)S(1)} %fusion, bf16[2,3072,1024]{2,1,0:T(8,128)(2,1)S(1)} %bitcast.89, bf16[1024,1,256]{2,0,1:T(8,128)(2,1)S(1)} %copy.20), kind=kOutput, calls=%fused_computation.31 | convolution fusion | flops 1611399168 | bytes 13107200 | tf_op jit(solution)/shard_map/dot_general | solution.py:12
  124.1 3.7 %fusion.17 = f32[1,16,16,3072]{3,2,1,0:T(8,128)S(1)} fusion(f32[16,3072,16]{1,2,0:T(8,128)S(1)} %fusion.56, f32[16,16,3072]{2,1,0:T(8,128)S(1)} %bitcast.84), kind=kOutput, calls=%fused_computation.21 | convolution fusion | flops 151785216 | bytes 9437184 | tf_op jit(solution)/shard_map/tm,rmc->rtc/dot_general | solution.py:36
  127.8 3.6 %fusion.16 = f32[1,16,16,3072]{3,2,1,0:T(8,128)S(1)} fusion(f32[16,3072,16]{1,2,0:T(8,128)S(1)} %fusion.52, f32[16,16,3072]{2,1,0:T(8,128)S(1)} %bitcast.85), kind=kOutput, calls=%fused_computation.19 | convolution fusion | flops 151785216 | bytes 9437184 | tf_op jit(solution)/shard_map/tm,rmc->rtc/dot_general | solution.py:36
  131.3 0.0 copy-start.1
  131.3 3.3 %pad_maximum_fusion = f32[2,16,16,3072]{3,2,1,0:T(8,128)} fusion(f32[1,16,16,3072]{3,2,1,0:T(8,128)S(1)} %fusion.16, f32[1,16,16,3072]{3,2,1,0:T(8,128)S(1)} %fusion.17), kind=kLoop, calls=%fused_computation | loop fusion | flops 1572864 | bytes 12582912 | tf_op jit(solution)/shard_map/stack | solution.py:40
  (14 shorter events, 0.1 us)
Async XLA Ops:
  6.5 26.2 %copy-start = (f32[8,1024]{1,0:T(8,128)S(1)}, f32[8,1024]{1,0:T(8,128)}, u32[]{:S(2)}) copy-start(f32[8,1024]{1,0:T(8,128)} %param.8) | copy-start | bytes 98308
  6.5 60.0 %reduce-scatter.2.cloned.1.call-start = ((), (), s32[]{:S(2)}) async-start(), calls=%async_computation.2 | async-start | bytes 2621440 | tf_op jit(solution)/shard_map/reduce_scatter | solution.py:56
  16.1 1.8 %copy-start.2 = (bf16[256,3072]{1,0:T(8,128)(2,1)S(1)}, bf16[256,3072]{1,0:T(8,128)(2,1)}, u32[]{:S(2)}) copy-start(bf16[256,3072]{1,0:T(8,128)(2,1)} %squeeze.36) | copy-start | bytes 4718596
  17.9 4.7 %copy-start.3 = (bf16[256,3072]{1,0:T(8,128)(2,1)S(1)}, bf16[256,3072]{1,0:T(8,128)(2,1)}, u32[]{:S(2)}) copy-start(bf16[256,3072]{1,0:T(8,128)(2,1)} %squeeze.16) | copy-start | bytes 4718596
  17.9 9.5 %slice-start = ((s8[12582912]{0:T(1024)(128)(4,1)}), s8[4194304]{0:T(1024)(128)(4,1)S(1)}, s32[]{:S(2)}) async-start(s8[12582912]{0:T(1024)(128)(4,1)} %bitcast.86), calls=%async_computation.4 | async-start | bytes 8388608
  17.9 9.5 %slice-start.1 = ((s8[12582912]{0:T(1024)(128)(4,1)}), s8[4194304]{0:T(1024)(128)(4,1)S(1)}, s32[]{:S(2)}) async-start(s8[12582912]{0:T(1024)(128)(4,1)} %bitcast.86), calls=%async_computation.5 | async-start | bytes 8388608
  22.6 4.8 %slice-start.2 = ((s8[12582912]{0:T(1024)(128)(4,1)}), s8[4194304]{0:T(1024)(128)(4,1)S(1)}, s32[]{:S(2)}) async-start(s8[12582912]{0:T(1024)(128)(4,1)} %bitcast.86), calls=%async_computation.6 | async-start | bytes 8388608
  31.0 1.5 %copy-start.4 = (s32[128]{0:T(128)S(1)}, s32[128]{0:T(128)}, u32[]{:S(2)}) copy-start(s32[128]{0:T(128)} %param.9) | copy-start | bytes 1540
  32.5 65.6 %all-gather.2.cloned.1.call-start = ((), (), s32[]{:S(2)}) async-start(), calls=%async_computation.3 | async-start | bytes 1310720 | tf_op jit(solution)/shard_map/all_gather | solution.py:79
  103.5 9.6 %slice-start.3 = ((s8[12582912]{0:T(1024)(128)(4,1)}), s8[4194304]{0:T(1024)(128)(4,1)S(1)}, s32[]{:S(2)}) async-start(s8[12582912]{0:T(1024)(128)(4,1)} %bitcast.88), calls=%async_computation.7 | async-start | bytes 8388608
  103.5 9.6 %slice-start.4 = ((s8[12582912]{0:T(1024)(128)(4,1)}), s8[4194304]{0:T(1024)(128)(4,1)S(1)}, s32[]{:S(2)}) async-start(s8[12582912]{0:T(1024)(128)(4,1)} %bitcast.88), calls=%async_computation.8 | async-start | bytes 8388608
  108.3 4.8 %slice-start.5 = ((s8[12582912]{0:T(1024)(128)(4,1)}), s8[4194304]{0:T(1024)(128)(4,1)S(1)}, s32[]{:S(2)}) async-start(s8[12582912]{0:T(1024)(128)(4,1)} %bitcast.88), calls=%async_computation.9 | async-start | bytes 8388608
  131.3 3.3 %copy-start.1 = (f32[8,1024]{1,0:T(8,128)S(1)}, f32[8,1024]{1,0:T(8,128)}, u32[]{:S(2)}) copy-start(f32[8,1024]{1,0:T(8,128)} %param.8) | copy-start | bytes 98308
Sparse Core Ops, SparseCore 0:
  32.6 33.8 reduce-scatter.1
  83.2 14.8 all-gather.1
where the time goes:
time: 142 us
  waiting for transfers between devices  48.5 us (34%)
  matrix products  41 us (29%)
  blocking collectives  14.1 us (10%)
  between operations  13.7 us (10%)
  local copies, waits for them, and re-layouts  12.6 us (9%)
  other arithmetic  11.6 us (8%)
    reduce_scatter x1, waiting for transfers between devices, shards(): lax.psum_scatter(mode_terms(masked_re, masked_im, kl_basis), 'freq', scat...  33.4 us
    dot_general x8, matrix products, product(): lax.dot_general(matrix, signal, contract_first, preferred_element_type=jn...  26.7 us
    all_gather x1, waiting for transfers between devices, shards(): lax.all_gather(coeffs, 'freq', axis=0, tiled=True)  15 us
    all_to_all x1, blocking collectives, shards(): lax.all_to_all(coeffs.reshape(held_modes, 2, real_count, local_m), 'ma',...  14.1 us
    dot_general x4, matrix products, apply_table(): jnp.einsum('tm,rmc->rtc', matrix, signal, precision=lax.Precision.HIGHEST)  14 us
    convert_element_type x1, other arithmetic, shards(): (visibility * column_mask).astype(jnp.bfloat16)  4.96 us
    slice x2, local copies, waits for them, and re-layouts, add_modes(): pieces[:, 0]  4.33 us
    another operation x1, other arithmetic, to_times(): return jnp.stack([series_re, series_im])  3.32 us
  transfers between devices with their start and end apart: 2, of which 2 were waited for; matrix products, arithmetic and copies ran while one was open for 0% of the time, Pallas kernels for 0%

commit v1 on v0

--- a/solution.py
+++ b/solution.py
@@ -76,7 +76,12 @@
         tiled=True,
     )
     coeffs = coeffs.reshape(held_modes, 2, -1)
-    fields_re, fields_im = add_modes(lax.all_gather(coeffs, "freq", axis=0, tiled=True), kl_basis)
+    fields_re, fields_im = add_modes(
+        jnp.concatenate(
+            lax.all_to_all(jnp.stack([coeffs] * lax.axis_size("freq")), "freq", 0, 0), axis=0
+        ),
+        kl_basis,
+    )
     fields = jnp.stack([fields_re, fields_im])
     return to_times(fields.reshape(2, real_count // lax.axis_size("ma"), -1, columns_dev))
 

time: 142 us -> 137 us (0.965)
  blocking collectives: 14.1 us -> 30.9 us
  waiting for transfers between devices: 48.5 us -> 33.5 us
  local copies, waits for them, and re-layouts: 12.6 us -> 6.82 us
    all_to_all x0 -> x1, blocking collectives: none -> 16.9 us  [shards(): lax.all_to_all(jnp.stack([coeffs] * lax.axis_size('freq')), 'freq', 0, 0)]
    all_gather x1 -> x0, waiting for transfers between devices: 15 us -> none  [shards(): lax.all_gather(coeffs, 'freq', axis=0, tiled=True)]
    slice x3 -> x0, local copies, waits for them, and re-layouts: 5.43 us -> none  [the longest x2 4.33 us: add_modes(): pieces[:, 0]]
  transfers between devices with their start and end apart: 2 -> 1, of which waited for: 2 -> 1; matrix products, arithmetic and copies ran while one was open for 0% -> 0% of each run, Pallas kernels for 0% -> 0%
where the time goes in v1:
time: 137 us
  matrix products  40.8 us (30%)
  waiting for transfers between devices  33.5 us (24%)
  blocking collectives  30.9 us (23%)
  between operations  13.7 us (10%)
  other arithmetic  11.4 us (8%)
  local copies, waits for them, and re-layouts  6.82 us (5%)
    reduce_scatter x1, waiting for transfers between devices, shards(): lax.psum_scatter(mode_terms(masked_re, masked_im, kl_basis), 'freq', scat...  33.5 us
    dot_general x8, matrix products, product(): lax.dot_general(matrix, signal, contract_first, preferred_element_type=jn...  26.6 us
    all_to_all x1, blocking collectives, shards(): lax.all_to_all(jnp.stack([coeffs] * lax.axis_size('freq')), 'freq', 0, 0)  16.9 us
    all_to_all x1, blocking collectives, shards(): lax.all_to_all(coeffs.reshape(held_modes, 2, real_count, local_m), 'ma',...  14.1 us
    dot_general x4, matrix products, apply_table(): jnp.einsum('tm,rmc->rtc', matrix, signal, precision=lax.Precision.HIGHEST)  13.9 us
    convert_element_type x1, other arithmetic, shards(): (visibility * column_mask).astype(jnp.bfloat16)  4.96 us
    another operation x1, other arithmetic, to_times(): return jnp.stack([series_re, series_im])  3.12 us
  transfers between devices with their start and end apart: 1, of which 1 were waited for; matrix products, arithmetic and copies ran while one was open for 0% of the time, Pallas kernels for 0%

profile of v1, /device:TPU:0, one launch (start us, length us, event | category | flops | bytes accessed | tf_op | source)
XLA Modules:
  0.0 137.1 jit_solution(12471110972971252353)
XLA Ops:
  6.5 0.0 copy-start
  6.5 0.0 reduce-scatter.2.cloned.1.call-start
  6.5 0.7 fusion.44
  7.3 0.1 reshape.44
  7.4 5.0 %multiply_convert_fusion = bf16[2,128,2,3072]{3,2,1,0:T(2,128)(2,1)S(1)} fusion(f32[2,128,2,3072]{3,2,1,0:T(2,128)} %param.5, f32[3072]{0:T(1024)S(1)} %reshape.44), kind=kLoop, calls=%fused_computation.17 | loop fusion | flops 3145728 | bytes 9449472 | tf_op jit(solution)/shard_map/convert_element_type | solution.py:51
  12.3 2.2 %fusion.89 = (bf16[1,128,2,3072]{3,2,1,0:T(2,128)(2,1)S(1)}, bf16[1,128,2,3072]{3,2,1,0:T(2,128)(2,1)S(1)}) fusion(bf16[2,128,2,3072]{3,2,1,0:T(2,128)(2,1)S(1)} %multiply_convert_fusion), kind=kLoop, calls=%fused_computation.88 | loop fusion | bytes 6291456 | tf_op jit(solution)/shard_map/slice | solution.py:53
  14.5 1.5 %squeeze.36 = bf16[256,3072]{1,0:T(8,128)(2,1)} reshape(bf16[1,128,2,3072]{3,2,1,0:T(2,128)(2,1)S(1)} %get-tuple-element.5) | data formatting | bytes 3145728 | tf_op jit(solution)/shard_map/squeeze | solution.py:53
  16.1 1.5 %squeeze.16 = bf16[256,3072]{1,0:T(8,128)(2,1)} reshape(bf16[1,128,2,3072]{3,2,1,0:T(2,128)(2,1)S(1)} %get-tuple-element.6) | data formatting | bytes 3145728 | tf_op jit(solution)/shard_map/squeeze | solution.py:52
  17.6 0.3 copy-done.2
  17.9 4.7 %fusion.6 = f32[256,1024]{1,0:T(8,128)S(1)} fusion(bf16[256,3072]{1,0:T(8,128)(2,1)S(1)} %copy-done.2, bf16[2,3072,1024]{2,1,0:T(8,128)(2,1)} %param.7), kind=kOutput, calls=%fused_computation.7 | convolution fusion | flops 1610612736 | bytes 8912896 | tf_op jit(solution)/shard_map/dot_general | solution.py:12
  22.6 0.0 copy-done.3
  22.6 0.0 slice-start.2
  22.6 4.7 %fusion.4 = f32[256,1024]{1,0:T(8,128)S(1)} fusion(bf16[256,3072]{1,0:T(8,128)(2,1)S(1)} %copy-done.3, bf16[2,3072,1024]{2,1,0:T(8,128)(2,1)} %param.7), kind=kOutput, calls=%fused_computation.5 | convolution fusion | flops 1610612736 | bytes 8912896 | tf_op jit(solution)/shard_map/dot_general | solution.py:12
  27.4 0.0 slice-done
  27.4 0.0 slice-done.1
  27.4 0.0 slice-done.2
  27.4 1.8 %fusion.35 = f32[1024,1,256]{0,2,1:T(8,128)S(1)} fusion(f32[256,1024]{1,0:T(8,128)S(1)} %fusion.6, bf16[256,3072]{1,0:T(8,128)(2,1)S(1)} %copy-done.3, bf16[2,3072,1024]{2,1,0:T(8,128)(2,1)S(1)} %bitcast.86), kind=kOutput, calls=%fused_computation.34 | convolution fusion | flops 1610874880 | bytes 9961472 | tf_op jit(solution)/shard_map/dot_general | solution.py:12
  29.2 1.8 %fusion.41 = f32[1024,1,256]{0,2,1:T(8,128)S(1)} fusion(f32[256,1024]{1,0:T(8,128)S(1)} %fusion.4, bf16[256,3072]{1,0:T(8,128)(2,1)S(1)} %copy-done.2, bf16[2,3072,1024]{2,1,0:T(8,128)(2,1)S(1)} %bitcast.86), kind=kOutput, calls=%fused_computation.36 | convolution fusion | flops 1610874880 | bytes 9961472 | tf_op jit(solution)/shard_map/dot_general | solution.py:12
  31.0 0.0 copy-start.4
  31.0 1.5 %pad_maximum_fusion.1 = f32[1024,2,256]{0,2,1:T(8,128)} fusion(f32[1024,1,256]{0,2,1:T(8,128)S(1)} %fusion.41, f32[1024,1,256]{0,2,1:T(8,128)S(1)} %fusion.35), kind=kLoop, calls=%fused_computation.32 | loop fusion | flops 524288 | bytes 4194304 | tf_op jit(solution)/shard_map/stack | solution.py:18
  32.5 0.0 reduce-scatter.2.cloned.1.call-update
  32.5 0.0 copy-done.4
  32.5 0.1 broadcast_in_dim.2
  32.6 0.1 eq.18
  32.7 0.3 fusion.56
  33.1 33.5 %reduce-scatter.2.cloned.1.call-done = f32[256,2,256]{0,2,1:T(8,128)} async-done(((f32[1024,2,256]{0,2,1:T(8,128)}), f32[256,2,256]{0,2,1:T(8,128)}) %reduce-scatter.2.cloned.1.call-update) | async-done | bytes 524304 | tf_op jit(solution)/shard_map/reduce_scatter | solution.py:56
  66.5 1.1 multiply_convert_fusion.1
  67.6 0.1 reshape.42
  67.7 0.2 copy.14
  67.9 14.1 %all_to_all.20 = bf16[256,2,128,2]{0,3,1,2:T(2,128)(2,1)S(1)} all-to-all(bf16[256,2,128,2]{0,3,1,2:T(2,128)(2,1)S(1)} %copy.14), channel_id=1, replica_groups=mesh['ma'=8,'freq'=4] {'ma'}, dimensions={2} | all-to-all | bytes 524288 | tf_op jit(solution)/shard_map/all_to_all | solution.py:71
  82.0 0.3 copy.16
  82.3 0.2 copy.17
  82.5 0.1 stack.27
  82.6 16.9 %all_to_all.21 = bf16[4,256,2,256]{3,1,2,0:T(8,128)(2,1)S(1)} all-to-all(bf16[4,256,2,256]{3,1,2,0:T(8,128)(2,1)S(1)} %stack.27), channel_id=1, replica_groups=mesh['ma'=8,'freq'=4] {'freq'}, dimensions={0} | all-to-all | bytes 2097152 | tf_op jit(solution)/shard_map/all_to_all | solution.py:81
  99.4 0.1 copy.18
  99.5 0.0 slice-start.3
  99.5 0.0 slice-start.4
  99.5 4.8 %fusion = f32[256,3072]{1,0:T(8,128)S(1)} fusion(bf16[2,3072,1024]{2,1,0:T(8,128)(2,1)} %param.7, bf16[1024,2,256]{2,0,1:T(8,128)(2,1)S(1)} %bitcast.89), kind=kOutput, calls=%fused_computation.1 | convolution fusion | flops 1610612736 | bytes 9961472 | tf_op jit(solution)/shard_map/dot_general | solution.py:12
  104.3 0.0 slice-start.5
  104.4 4.8 %fusion.2 = f32[256,3072]{1,0:T(8,128)S(1)} fusion(bf16[2,3072,1024]{2,1,0:T(8,128)(2,1)} %param.7, bf16[1024,2,256]{2,0,1:T(8,128)(2,1)S(1)} %bitcast.90), kind=kOutput, calls=%fused_computation.3 | convolution fusion | flops 1610612736 | bytes 9961472 | tf_op jit(solution)/shard_map/dot_general | solution.py:12
  109.2 1.8 %fusion.26 = f32[256,3072]{1,0:T(8,128)S(1)} fusion(f32[256,3072]{1,0:T(8,128)S(1)} %fusion.2, bf16[2,3072,1024]{2,1,0:T(8,128)(2,1)S(1)} %bitcast.88, bf16[1024,2,256]{2,0,1:T(8,128)(2,1)S(1)} %bitcast.91), kind=kOutput, calls=%fused_computation.30 | convolution fusion | flops 1611399168 | bytes 13107200 | tf_op jit(solution)/shard_map/dot_general | solution.py:12
  111.1 3.4 %fusion.48 = f32[16,3072,16]{1,2,0:T(8,128)S(1)} fusion(f32[16,16,3072]{2,1,0:T(8,128)S(1)} %bitcast.81), kind=kOutput, calls=%fused_computation.48 | convolution fusion | flops 150998784 | bytes 6291456 | tf_op jit(solution)/shard_map/tm,rmc->rtc/dot_general | solution.py:36
  114.4 3.4 %fusion.52 = f32[16,3072,16]{1,2,0:T(8,128)S(1)} fusion(f32[16,16,3072]{2,1,0:T(8,128)S(1)} %bitcast.82), kind=kOutput, calls=%fused_computation.52 | convolution fusion | flops 150998784 | bytes 6291456 | tf_op jit(solution)/shard_map/tm,rmc->rtc/dot_general | solution.py:36
  117.9 2.1 %fusion.29 = f32[256,3072]{1,0:T(8,128)S(1)} fusion(f32[256,3072]{1,0:T(8,128)S(1)} %fusion, bf16[2,3072,1024]{2,1,0:T(8,128)(2,1)S(1)} %bitcast.88, bf16[1024,2,256]{2,0,1:T(8,128)(2,1)S(1)} %bitcast.92), kind=kOutput, calls=%fused_computation.31 | convolution fusion | flops 1611399168 | bytes 13107200 | tf_op jit(solution)/shard_map/dot_general | solution.py:12
  120.0 3.6 %fusion.17 = f32[1,16,16,3072]{3,2,1,0:T(8,128)S(1)} fusion(f32[16,3072,16]{1,2,0:T(8,128)S(1)} %fusion.52, f32[16,16,3072]{2,1,0:T(8,128)S(1)} %bitcast.83), kind=kOutput, calls=%fused_computation.21 | convolution fusion | flops 151785216 | bytes 9437184 | tf_op jit(solution)/shard_map/tm,rmc->rtc/dot_general | solution.py:36
  123.5 3.6 %fusion.16 = f32[1,16,16,3072]{3,2,1,0:T(8,128)S(1)} fusion(f32[16,3072,16]{1,2,0:T(8,128)S(1)} %fusion.48, f32[16,16,3072]{2,1,0:T(8,128)S(1)} %bitcast.84), kind=kOutput, calls=%fused_computation.19 | convolution fusion | flops 151785216 | bytes 9437184 | tf_op jit(solution)/shard_map/tm,rmc->rtc/dot_general | solution.py:36
  127.1 0.0 copy-start.1
  127.1 3.1 %pad_maximum_fusion = f32[2,16,16,3072]{3,2,1,0:T(8,128)} fusion(f32[1,16,16,3072]{3,2,1,0:T(8,128)S(1)} %fusion.16, f32[1,16,16,3072]{3,2,1,0:T(8,128)S(1)} %fusion.17), kind=kLoop, calls=%fused_computation | loop fusion | flops 1572864 | bytes 12582912 | tf_op jit(solution)/shard_map/stack | solution.py:40
  (12 shorter events, 0.0 us)
Async XLA Ops:
  6.5 26.2 %copy-start = (f32[8,1024]{1,0:T(8,128)S(1)}, f32[8,1024]{1,0:T(8,128)}, u32[]{:S(2)}) copy-start(f32[8,1024]{1,0:T(8,128)} %param.8) | copy-start | bytes 98308
  6.5 60.0 %reduce-scatter.2.cloned.1.call-start = ((), (), s32[]{:S(2)}) async-start(), calls=%async_computation.3 | async-start | bytes 2621440 | tf_op jit(solution)/shard_map/reduce_scatter | solution.py:56
  16.1 1.8 %copy-start.2 = (bf16[256,3072]{1,0:T(8,128)(2,1)S(1)}, bf16[256,3072]{1,0:T(8,128)(2,1)}, u32[]{:S(2)}) copy-start(bf16[256,3072]{1,0:T(8,128)(2,1)} %squeeze.36) | copy-start | bytes 4718596
  17.9 4.7 %copy-start.3 = (bf16[256,3072]{1,0:T(8,128)(2,1)S(1)}, bf16[256,3072]{1,0:T(8,128)(2,1)}, u32[]{:S(2)}) copy-start(bf16[256,3072]{1,0:T(8,128)(2,1)} %squeeze.16) | copy-start | bytes 4718596
  17.9 9.5 %slice-start = ((s8[12582912]{0:T(1024)(128)(4,1)}), s8[4194304]{0:T(1024)(128)(4,1)S(1)}, s32[]{:S(2)}) async-start(s8[12582912]{0:T(1024)(128)(4,1)} %bitcast.85), calls=%async_computation.4 | async-start | bytes 8388608
  17.9 9.5 %slice-start.1 = ((s8[12582912]{0:T(1024)(128)(4,1)}), s8[4194304]{0:T(1024)(128)(4,1)S(1)}, s32[]{:S(2)}) async-start(s8[12582912]{0:T(1024)(128)(4,1)} %bitcast.85), calls=%async_computation.5 | async-start | bytes 8388608
  22.6 4.8 %slice-start.2 = ((s8[12582912]{0:T(1024)(128)(4,1)}), s8[4194304]{0:T(1024)(128)(4,1)S(1)}, s32[]{:S(2)}) async-start(s8[12582912]{0:T(1024)(128)(4,1)} %bitcast.85), calls=%async_computation.6 | async-start | bytes 8388608
  31.0 1.5 %copy-start.4 = (s32[128]{0:T(128)S(1)}, s32[128]{0:T(128)}, u32[]{:S(2)}) copy-start(s32[128]{0:T(128)} %param.9) | copy-start | bytes 1540
  99.5 9.7 %slice-start.3 = ((s8[12582912]{0:T(1024)(128)(4,1)}), s8[4194304]{0:T(1024)(128)(4,1)S(1)}, s32[]{:S(2)}) async-start(s8[12582912]{0:T(1024)(128)(4,1)} %bitcast.87), calls=%async_computation.7 | async-start | bytes 8388608
  99.5 9.7 %slice-start.4 = ((s8[12582912]{0:T(1024)(128)(4,1)}), s8[4194304]{0:T(1024)(128)(4,1)S(1)}, s32[]{:S(2)}) async-start(s8[12582912]{0:T(1024)(128)(4,1)} %bitcast.87), calls=%async_computation.8 | async-start | bytes 8388608
  104.3 4.9 %slice-start.5 = ((s8[12582912]{0:T(1024)(128)(4,1)}), s8[4194304]{0:T(1024)(128)(4,1)S(1)}, s32[]{:S(2)}) async-start(s8[12582912]{0:T(1024)(128)(4,1)} %bitcast.87), calls=%async_computation.9 | async-start | bytes 8388608
  127.1 3.1 %copy-start.1 = (f32[8,1024]{1,0:T(8,128)S(1)}, f32[8,1024]{1,0:T(8,128)}, u32[]{:S(2)}) copy-start(f32[8,1024]{1,0:T(8,128)} %param.8) | copy-start | bytes 98308
Sparse Core Ops, SparseCore 0:
  32.6 33.8 reduce-scatter.1
